TPU v7x, 256 devices: a whole 4x4x8 slice. The times are simulated.
256 devices in a mesh: row: 32 (over x, z_hi, core), col: 8 (over y, z_lo).
Axes of the slice: x: 4, y: 4, z: 8 (z_hi: 4, z_lo: 2; z = z_hi * 2 + z_lo), core: 2. Of those that a mesh axis runs over, the one named last changes fastest.
Arguments:
- ancestor_inverse: bfloat16 [24576, 8, 3072], P('row', 'col'), may hold values from -6 to 6
- parent_panel: bfloat16 [24576, 1024], P(('row', 'col')), may hold values from -0.15625 to 0.15625
- parent_diag_inv: bfloat16 [1024, 1024], replicated, may hold values from -1.5 to 1.5, as said below
- child_panel_anc: bfloat16 [24576, 1024], P(('row', 'col')), may hold values from -0.15625 to 0.15625
- child_panel_par: bfloat16 [1024, 1024], replicated, may hold values from -0.1875 to 0.1875
- child_diag_inv: bfloat16 [1024, 1024], replicated, may hold values from -1.5 to 1.5, as said below
Outputs:
- ainv_ap: float32 [24576, 1024], P(('row', 'col'))
- ainv_pp: float32 [1024, 1024], P(('row', 'col'))
- ainv_ac: float32 [24576, 1024], P(('row', 'col'))
- ainv_pc: float32 [1024, 1024], P(('row', 'col'))
- ainv_cc: float32 [1024, 1024], P(('row', 'col'))
Inputs may be any that keep to these rules, and one draw needn't show every extreme that they name: `parent_diag_inv`: lower triangular, with diagonal entries between 0.5 and 1.5. `child_diag_inv`: lower triangular, with diagonal entries between 0.5 and 1.5.
All inputs are finite; a program needn't handle non-finite values.
Results may differ from a plain program's by a relative error of at most 0.0041.
Values may be sent and summed in bfloat16 or wider, within the bound.
No kernel may reach another device: no remote copies, remote signals or barrier semaphores. Data moves between devices by JAX's collectives and lax.ppermute only.
A program may use at most 128 MiB of HBM per device.

v0:
```python
import jax
import jax.numpy as jnp
from jax import lax
from jax.sharding import PartitionSpec as P


def contract_rows(left_side, right_side):
    return lax.dot_general(
        left_side, right_side, (((0,), (0,)), ((), ())), preferred_element_type=jnp.float32
    )


def shards(
    ancestor_inverse,
    parent_panel,
    parent_diag_inv,
    child_panel_anc,
    child_panel_par,
    child_diag_inv,
):
    local_rows = ancestor_inverse.shape[0]
    local_block = ancestor_inverse.reshape(local_rows, -1)
    columns = parent_panel.shape[1]

    def add_panel(pieces):
        return jnp.dot(local_block, pieces, preferred_element_type=jnp.float32)

    pieces = (
        lax.all_gather(parent_panel, "row", axis=0, tiled=True),
        lax.all_gather(child_panel_anc, "row", axis=0, tiled=True),
    )
    partial_upper = add_panel(pieces[0])
    partial_lower = add_panel(pieces[1])
    upper_prod, lower_first = (
        lax.psum_scatter(partial_upper, "col", scatter_dimension=0, tiled=True),
        lax.psum_scatter(partial_lower, "col", scatter_dimension=0, tiled=True),
    )
    upper_round = upper_prod.astype(jnp.bfloat16)
    shifted = jnp.dot(upper_round, child_panel_par, preferred_element_type=jnp.float32)
    shifted_round = shifted.astype(jnp.bfloat16)
    lower_prod_anc = lower_first - shifted
    anc_round = lower_prod_anc.astype(jnp.bfloat16)
    mixed_round = jnp.dot(parent_panel, child_panel_par, preferred_element_type=jnp.float32).astype(
        jnp.bfloat16
    )
    diag_prod = jnp.dot(
        parent_diag_inv, child_panel_par, preferred_element_type=jnp.float32
    ).astype(jnp.bfloat16)
    devices = lax.axis_size("row") * lax.axis_size("col")
    my_rows = columns // devices
    position = lax.axis_index("row") * lax.axis_size("col") + lax.axis_index("col")
    first_row = position * my_rows
    parent_cols = lax.dynamic_slice_in_dim(parent_diag_inv, first_row, my_rows, 1)
    diag_upper = contract_rows(parent_cols, parent_diag_inv)
    child_cols = lax.dynamic_slice_in_dim(child_diag_inv, first_row, my_rows, 1)
    prod_cols = lax.dynamic_slice_in_dim(diag_prod, first_row, my_rows, 1)
    diag_lower = contract_rows(child_cols, child_diag_inv) + contract_rows(prod_cols, diag_prod)
    from_anc = contract_rows(child_panel_anc, anc_round)
    from_mixed = contract_rows(mixed_round, shifted_round)
    from_shift = contract_rows(shifted_round, child_panel_anc)
    joined_sum = lax.psum_scatter(
        jnp.concatenate(
            [
                contract_rows(parent_panel, upper_round),
                contract_rows(upper_round, child_panel_anc),
                from_anc + from_mixed - from_shift,
            ],
            axis=1,
        ),
        ("row", "col"),
        scatter_dimension=0,
        tiled=True,
    )
    upper_sum = joined_sum[:, :columns]
    cross_sum = joined_sum[:, columns : 2 * columns]
    lower_sum = joined_sum[:, 2 * columns :]
    ainv_pp = diag_upper + upper_sum
    pp_round = ainv_pp.astype(jnp.bfloat16)
    lower_prod_par = (
        jnp.dot(pp_round, child_panel_par, preferred_element_type=jnp.float32) - cross_sum
    )
    ainv_cc = diag_lower + lower_sum
    return (-upper_prod, ainv_pp, -lower_prod_anc, -lower_prod_par, ainv_cc)


def solution(mesh):
    placed = (
        P("row", "col", None),
        P(("row", "col"), None),
        P(),
        P(("row", "col"), None),
        P(),
        P(),
    )
    return jax.shard_map(
        shards,
        mesh=mesh,
        in_specs=placed,
        out_specs=(
            P(("row", "col"), None),
            P(("row", "col"), None),
            P(("row", "col"), None),
            P(("row", "col"), None),
            P(("row", "col"), None),
        ),
        check_vma=False,
    )
```

profile of v0, /device:TPU:8, one launch (start us, length us, event | category | flops | bytes accessed | tf_op | source)
XLA Modules:
  0.0 634.1 jit_solution(10543304892223463329)
XLA Ops:
  8.0 0.7 all-gather.5.cloned.1.call-update
  8.7 73.7 %all-gather.3.cloned.1.call-done = bf16[3072,1024]{1,0:T(8,128)(2,1)} async-done(((bf16[96,1024]{1,0:T(8,128)(2,1)}), bf16[3072,1024]{1,0:T(8,128)(2,1)}) %all-gather.3.cloned.1.call-update) | async-done | bytes 6291472 | tf_op jit(solution)/shard_map/all_gather | solution.py:29
  82.4 9.7 %fusion.2 = f32[768,1024]{1,0:T(8,128)} fusion(bf16[3072,1024]{1,0:T(8,128)(2,1)} %all-gather.3.cloned.1.call-done, bf16[768,1,3072]{2,0,1:T(8,128)(2,1)} %param.6), kind=kOutput, calls=%fused_computation.3 | convolution fusion | flops 4831838208 | bytes 14155776 | tf_op jit(solution)/shard_map/dot_general | solution.py:26
  92.2 59.7 %all-gather.5.cloned.1.call-done = bf16[3072,1024]{1,0:T(8,128)(2,1)} async-done(((bf16[96,1024]{1,0:T(8,128)(2,1)}), bf16[3072,1024]{1,0:T(8,128)(2,1)}) %all-gather.5.cloned.1.call-update) | async-done | bytes 6291472 | tf_op jit(solution)/shard_map/all_gather | solution.py:30
  151.9 9.7 %fusion = f32[768,1024]{1,0:T(8,128)} fusion(bf16[3072,1024]{1,0:T(8,128)(2,1)} %all-gather.5.cloned.1.call-done, bf16[768,1,3072]{2,0,1:T(8,128)(2,1)} %param.6), kind=kOutput, calls=%fused_computation.1 | convolution fusion | flops 4831838208 | bytes 14155776 | tf_op jit(solution)/shard_map/dot_general | solution.py:26
  161.9 63.8 %reduce-scatter.3.cloned.1.call-done = f32[96,1024]{1,0:T(8,128)} async-done(((f32[768,1024]{1,0:T(8,128)}), f32[96,1024]{1,0:T(8,128)}) %reduce-scatter.3.cloned.1.call-update) | async-done | bytes 393232 | tf_op jit(solution)/shard_map/reduce_scatter | solution.py:35
  225.7 76.5 %reduce-scatter.5.cloned.1.call-done = f32[96,1024]{1,0:T(8,128)} async-done(((f32[768,1024]{1,0:T(8,128)}), f32[96,1024]{1,0:T(8,128)}) %reduce-scatter.5.cloned.1.call-update) | async-done | bytes 393232 | tf_op jit(solution)/shard_map/reduce_scatter | solution.py:36
  302.1 2.3 subtract_negate_fusion
  304.5 2.7 fusion.13
  307.2 3.0 fusion.5
  310.2 0.7 convolution_bitcast_fusion
  311.0 0.8 fusion.23
  311.7 0.7 copy-done.1
  312.4 1.3 copy-done.2
  313.7 0.9 fusion.4
  314.6 5.6 pad_maximum_fusion
  320.2 12.6 %copy.16 = f32[1024,3072]{1,0:T(8,128)} copy(f32[1024,3072]{0,1:T(8,128)} %pad_maximum_fusion) | data formatting | bytes 25165824 | tf_op jit(solution)/shard_map/concatenate | solution.py:62
  332.9 2.2 fusion.8
  335.0 5.4 convolution_convert_fusion
  340.4 0.8 neg.9
  341.2 280.3 %all-reduce.3.cloned.1.call-done = f32[1024,3072]{1,0:T(8,128)} async-done(((f32[1024,3072]{1,0:T(8,128)}), f32[1024,3072]{1,0:T(8,128)}) %all-reduce.3.cloned.1.call-update) | async-done | bytes 12582928
  621.5 2.2 convolution_add_fusion.1
  623.7 1.8 fusion.7
  625.5 2.0 fusion.6
  (25 shorter events, 1.1 us)
Async XLA Ops:
  7.2 295.0 %copy-start = (bf16[1024,1024]{1,0:T(8,128)(2,1)S(1)}, bf16[1024,1024]{1,0:T(8,128)(2,1)}, u32[]{:S(2)}) copy-start(bf16[1024,1024]{1,0:T(8,128)(2,1)} %param.10) | copy-start | bytes 6291460
  7.2 75.2 %all-gather.3.cloned.1.call-start = ((), (), s32[]{:S(2)}) async-start(), calls=%async_computation.2 | async-start | bytes 6488064 | tf_op jit(solution)/shard_map/all_gather | solution.py:29
  7.9 144.0 %all-gather.5.cloned.1.call-start = ((), (), s32[]{:S(2)}) async-start(), calls=%async_computation.4 | async-start | bytes 6488064 | tf_op jit(solution)/shard_map/all_gather | solution.py:30
  8.7 217.0 %reduce-scatter.3.cloned.1.call-start = ((), (), s32[]{:S(2)}) async-start(), calls=%async_computation.3 | async-start | bytes 3538944 | tf_op jit(solution)/shard_map/reduce_scatter | solution.py:35
  92.1 210.0 %reduce-scatter.5.cloned.1.call-start = ((), (), s32[]{:S(2)}) async-start(), calls=%async_computation.5 | async-start | bytes 3538944 | tf_op jit(solution)/shard_map/reduce_scatter | solution.py:36
  161.6 142.9 %copy-start.4 = (bf16[96,1024]{1,0:T(8,128)(2,1)S(1)}, bf16[96,1024]{1,0:T(8,128)(2,1)}, u32[]{:S(2)}) copy-start(bf16[96,1024]{1,0:T(8,128)(2,1)} %param.9) | copy-start | bytes 589828
  161.6 145.6 %copy-start.6 = (bf16[96,1024]{1,0:T(8,128)(2,1)S(1)}, bf16[96,1024]{1,0:T(8,128)(2,1)}, u32[]{:S(2)}) copy-start(bf16[96,1024]{1,0:T(8,128)(2,1)} %param.7) | copy-start | bytes 589828
  161.6 459.9 %all-reduce.3.cloned.1.call-start = ((), (), s32[]{:S(2)}) async-start(), calls=%async_computation.6 | async-start | bytes 25165824
  307.2 3.0 copy-start.3
  310.2 2.2 copy-start.1
  310.2 3.5 copy-start.2
  310.2 3.5 copy-start.7
  621.5 4.0 copy-start.5
  623.7 3.8 copy-start.8
Sparse Core Ops, SparseCore 0:
  10.6 71.7 all-gather.2
  84.9 66.9 all-gather.4
  154.5 71.1 reduce-scatter.2
  228.1 74.0 reduce-scatter.4
  333.0 288.4 all-reduce.2
where the time goes:
time: 635 us; the launch traced here: 634 us
  waiting for transfers between devices  555 us (87%)
  matrix products  43.4 us (7%)
  local copies, waits for them, and re-layouts  14.6 us (2%)
  between operations  13.8 us (2%)
  other arithmetic  6.41 us (1%)
    unnamed x6, waiting for transfers between devices  282 us
    reduce_scatter x1, waiting for transfers between devices, shards(): lax.psum_scatter(partial_lower, 'col', scatter_dimension=0, tiled=True)  76.5 us
    all_gather x1, waiting for transfers between devices, shards(): lax.all_gather(parent_panel, 'row', axis=0, tiled=True)  73.7 us
    reduce_scatter x1, waiting for transfers between devices, shards(): lax.psum_scatter(partial_upper, 'col', scatter_dimension=0, tiled=True)  63.8 us
    all_gather x1, waiting for transfers between devices, shards(): lax.all_gather(child_panel_anc, 'row', axis=0, tiled=True)  59.7 us
    dot_general x2, matrix products, add_panel(): return jnp.dot(local_block, pieces, preferred_element_type=jnp.float32)  19.4 us
    dot_general x8, matrix products, contract_rows(): lax.dot_general(left_side, right_side, (((0,), (0,)), ((), ())), preferre...  14.5 us
  transfers between devices with their start and end apart: 5, of which 5 were waited for; matrix products, arithmetic and copies ran while one was open for 4% of the time, Pallas kernels for 0%

commit v1 on v0

--- a/solution.py
+++ b/solution.py
@@ -27,7 +27,9 @@
 
     pieces = (
         lax.all_gather(parent_panel, "row", axis=0, tiled=True),
-        lax.all_gather(child_panel_anc, "row", axis=0, tiled=True),
+        jnp.concatenate(
+            lax.all_to_all(jnp.stack([child_panel_anc] * lax.axis_size("row")), "row", 0, 0), axis=0
+        ),
     )
     partial_upper = add_panel(pieces[0])
     partial_lower = add_panel(pieces[1])

time: 635 us -> 672 us (1.058)
  waiting for transfers between devices: 555 us -> 578 us
  starting transfers between devices: 0.38 us -> 11.8 us
    all_gather x1, waiting for transfers between devices: 73.7 us -> 155 us  [shards(): lax.all_gather(parent_panel, 'row', axis=0, tiled=True)]
    all_gather x1 -> x0, waiting for transfers between devices: 59.7 us -> none  [shards(): lax.all_gather(child_panel_anc, 'row', axis=0, tiled=True)]
    all_to_all x0 -> x1, starting transfers between devices: none -> 11.4 us  [shards(): lax.all_to_all(jnp.stack([child_panel_anc] * lax.axis_size('row')), 'row'...]
    unnamed x6 -> x5, waiting for transfers between devices: 282 us -> 282 us
  transfers between devices with their start and end apart: 5 -> 5, of which waited for: 5 -> 5; matrix products, arithmetic and copies ran while one was open for 4% -> 5% of each run, Pallas kernels for 0% -> 0%
where the time goes in v1:
time: 672 us
  waiting for transfers between devices  578 us (86%)
  matrix products  43.4 us (6%)
  local copies, waits for them, and re-layouts  19 us (3%)
  between operations  13.8 us (2%)
  starting transfers between devices  11.8 us (2%)
    unnamed x5, waiting for transfers between devices  282 us
    all_gather x1, waiting for transfers between devices, shards(): lax.all_gather(parent_panel, 'row', axis=0, tiled=True)  155 us
    reduce_scatter x1, waiting for transfers between devices, shards(): lax.psum_scatter(partial_lower, 'col', scatter_dimension=0, tiled=True)  76.6 us
    reduce_scatter x1, waiting for transfers between devices, shards(): lax.psum_scatter(partial_upper, 'col', scatter_dimension=0, tiled=True)  58.5 us
    dot_general x2, matrix products, add_panel(): return jnp.dot(local_block, pieces, preferred_element_type=jnp.float32)  19.4 us
    dot_general x8, matrix products, contract_rows(): lax.dot_general(left_side, right_side, (((0,), (0,)), ((), ())), preferre...  14.5 us
  transfers between devices with their start and end apart: 5, of which 5 were waited for; matrix products, arithmetic and copies ran while one was open for 5% of the time, Pallas kernels for 0%

profile of v1, /device:TPU:8, one launch (start us, length us, event | category | flops | bytes accessed | tf_op | source)
XLA Modules:
  0.0 671.9 jit_solution(17013988099500970660)
XLA Ops:
  7.9 4.4 stack.2
  12.3 11.4 %all-to-all-start = ((bf16[32,96,1024]{2,1,0:T(8,128)(2,1)}), bf16[32,96,1024]{2,1,0:T(8,128)(2,1)}, u32[]{:S(2)}, u32[]{:S(2)}) async-start(bf16[32,96,1024]{2,1,0:T(8,128)(2,1)} %stack.2), calls=%async_computation.1 | async-start | bytes 12582912 | tf_op jit(solution)/shard_map/all_to_all | solution.py:31
  23.8 155.4 %all-gather.2.cloned.1.call-done = bf16[3072,1024]{1,0:T(8,128)(2,1)} async-done(((bf16[96,1024]{1,0:T(8,128)(2,1)}), bf16[3072,1024]{1,0:T(8,128)(2,1)}) %all-gather.2.cloned.1.call-update) | async-done | bytes 6291472 | tf_op jit(solution)/shard_map/all_gather | solution.py:29
  179.1 9.7 %fusion.2 = f32[768,1024]{1,0:T(8,128)} fusion(bf16[3072,1024]{1,0:T(8,128)(2,1)} %all-gather.2.cloned.1.call-done, bf16[768,1,3072]{2,0,1:T(8,128)(2,1)} %param.6), kind=kOutput, calls=%fused_computation.3 | convolution fusion | flops 4831838208 | bytes 14155776 | tf_op jit(solution)/shard_map/dot_general | solution.py:26
  188.9 5.4 all-to-all-done
  194.4 9.7 %fusion = f32[768,1024]{1,0:T(8,128)} fusion(bf16[3072,1024]{1,0:T(8,128)(2,1)} %bitcast.2, bf16[768,1,3072]{2,0,1:T(8,128)(2,1)} %param.6), kind=kOutput, calls=%fused_computation.1 | convolution fusion | flops 4831838208 | bytes 14155776 | tf_op jit(solution)/shard_map/dot_general | solution.py:26
  204.3 58.5 %reduce-scatter.3.cloned.1.call-done = f32[96,1024]{1,0:T(8,128)} async-done(((f32[768,1024]{1,0:T(8,128)}), f32[96,1024]{1,0:T(8,128)}) %reduce-scatter.3.cloned.1.call-update) | async-done | bytes 393232 | tf_op jit(solution)/shard_map/reduce_scatter | solution.py:37
  262.9 76.6 %reduce-scatter.5.cloned.1.call-done = f32[96,1024]{1,0:T(8,128)} async-done(((f32[768,1024]{1,0:T(8,128)}), f32[96,1024]{1,0:T(8,128)}) %reduce-scatter.5.cloned.1.call-update) | async-done | bytes 393232 | tf_op jit(solution)/shard_map/reduce_scatter | solution.py:38
  339.5 2.3 subtract_negate_fusion
  341.9 2.7 fusion.13
  344.6 3.0 fusion.5
  347.6 0.7 convolution_bitcast_fusion
  348.3 0.8 fusion.23
  349.8 1.3 copy-done.2
  351.1 0.9 fusion.4
  351.9 5.6 pad_maximum_fusion
  357.5 12.6 %copy.16 = f32[1024,3072]{1,0:T(8,128)} copy(f32[1024,3072]{0,1:T(8,128)} %pad_maximum_fusion) | data formatting | bytes 25165824 | tf_op jit(solution)/shard_map/concatenate | solution.py:64
  370.2 2.2 fusion.8
  372.3 5.4 convolution_convert_fusion
  377.7 0.8 neg.9
  378.5 280.9 %all-reduce.3.cloned.1.call-done = f32[1024,3072]{1,0:T(8,128)} async-done(((f32[1024,3072]{1,0:T(8,128)}), f32[1024,3072]{1,0:T(8,128)}) %all-reduce.3.cloned.1.call-update) | async-done | bytes 12582928
  659.4 2.2 convolution_add_fusion.1
  661.6 1.8 fusion.7
  663.4 2.0 fusion.6
  (25 shorter events, 1.8 us)
Async XLA Ops:
  7.2 332.4 %copy-start = (bf16[1024,1024]{1,0:T(8,128)(2,1)S(1)}, bf16[1024,1024]{1,0:T(8,128)(2,1)}, u32[]{:S(2)}) copy-start(bf16[1024,1024]{1,0:T(8,128)(2,1)} %param.10) | copy-start | bytes 6291460
  7.2 172.0 %all-gather.2.cloned.1.call-start = ((), (), s32[]{:S(2)}) async-start(), calls=%async_computation.3 | async-start | bytes 6488064 | tf_op jit(solution)/shard_map/all_gather | solution.py:29
  12.3 182.1 %all-to-all-start = ((bf16[32,96,1024]{2,1,0:T(8,128)(2,1)}), bf16[32,96,1024]{2,1,0:T(8,128)(2,1)}, u32[]{:S(2)}, u32[]{:S(2)}) async-start(bf16[32,96,1024]{2,1,0:T(8,128)(2,1)} %stack.2), calls=%async_computation.1 | async-start | bytes 12582912 | tf_op jit(solution)/shard_map/all_to_all | solution.py:31
  23.7 239.2 %reduce-scatter.3.cloned.1.call-start = ((), (), s32[]{:S(2)}) async-start(), calls=%async_computation.4 | async-start | bytes 3538944 | tf_op jit(solution)/shard_map/reduce_scatter | solution.py:37
  188.9 150.7 %reduce-scatter.5.cloned.1.call-start = ((), (), s32[]{:S(2)}) async-start(), calls=%async_computation.5 | async-start | bytes 3538944 | tf_op jit(solution)/shard_map/reduce_scatter | solution.py:38
  204.1 137.8 %copy-start.4 = (bf16[96,1024]{1,0:T(8,128)(2,1)S(1)}, bf16[96,1024]{1,0:T(8,128)(2,1)}, u32[]{:S(2)}) copy-start(bf16[96,1024]{1,0:T(8,128)(2,1)} %param.9) | copy-start | bytes 589828
  204.1 140.5 %copy-start.6 = (bf16[96,1024]{1,0:T(8,128)(2,1)S(1)}, bf16[96,1024]{1,0:T(8,128)(2,1)}, u32[]{:S(2)}) copy-start(bf16[96,1024]{1,0:T(8,128)(2,1)} %param.7) | copy-start | bytes 589828
  204.1 455.3 %all-reduce.3.cloned.1.call-start = ((), (), s32[]{:S(2)}) async-start(), calls=%async_computation.6 | async-start | bytes 25165824
  344.6 3.0 copy-start.3
  347.6 2.2 copy-start.1
  347.6 3.5 copy-start.2
  347.6 3.5 copy-start.7
  659.4 4.0 copy-start.5
  661.6 3.8 copy-start.8
Sparse Core Ops, SparseCore 0:
  10.6 168.5 all-gather.1
  189.0 73.8 reduce-scatter.2
  265.5 74.0 reduce-scatter.4
  370.3 289.0 all-reduce.2
